TPU v7x, 512 devices: a whole 4x8x8 slice. The times are simulated.
512 devices in a mesh: dp: 8 (over z_hi, x), expert: 64 (over y, z_lo, core).
Axes of the slice: x: 4, y: 8, z: 8 (z_hi: 2, z_lo: 4; z = z_hi * 4 + z_lo), core: 2. Of those that a mesh axis runs over, the one named last changes fastest.
Arguments:
- tokens: bfloat16 [65536, 1024], P(('dp', 'expert')), may hold values from -6 to 6
- cotangent: bfloat16 [65536, 1024], P(('dp', 'expert')), may hold values from -6 to 6
- pick_lists: int32 [8, 64, 128], P('dp'), may hold values from 0 to 8191, as said below
- combine: float32 [8, 64, 128], P('dp'), may hold values from 0.1 to 1
- w_gate: bfloat16 [64, 1024, 1024], P('expert', 'dp'), may hold values from -0.1875 to 0.1875
- w_up: bfloat16 [64, 1024, 1024], P('expert', 'dp'), may hold values from -0.1875 to 0.1875
- w_down: bfloat16 [64, 1024, 1024], P('expert', 'dp'), may hold values from -0.1875 to 0.1875
Outputs:
- layer_out: bfloat16 [65536, 1024], P(('dp', 'expert'))
- tokens_grad: bfloat16 [65536, 1024], P(('dp', 'expert'))
- grad_gate: bfloat16 [64, 1024, 1024], P('expert', 'dp')
- grad_up: bfloat16 [64, 1024, 1024], P('expert', 'dp')
- grad_down: bfloat16 [64, 1024, 1024], P('expert', 'dp')
Inputs may be any that keep to these rules, and one draw needn't show every extreme that they name: Each list pick_lists[r, e] names 128 distinct tokens of replica r. Token numbers j * 128 to (j + 1) * 128 - 1 are those of the device with index j on the expert axis; at most 4 picks of one expert in one replica fall among one device's tokens, and for every expert and replica exactly 4 fall among some device's.
All inputs are finite; a program needn't handle non-finite values.
Results may differ from a plain program's by a relative error of at most 0.013.
Values may be sent and summed in bfloat16 or wider, within the bound.
No kernel may reach another device: no remote copies, remote signals or barrier semaphores. Data moves between devices by JAX's collectives and lax.ppermute only.
A program may use at most 64 MiB of HBM per device.

v0:
```python
import jax
import jax.numpy as jnp
from jax import lax
from jax.sharding import PartitionSpec as P


def silu_parts(gate_pre):
    sigma_gate = jax.nn.sigmoid(gate_pre)
    return (gate_pre * sigma_gate, sigma_gate)


def project_hidden(row_block, gate_w, up_w):
    dims = (((1,), (1,)), ((), ()))
    gate_pre = lax.dot_general(row_block, gate_w, dims, preferred_element_type=jnp.float32)
    up_pre = lax.dot_general(row_block, up_w, dims, preferred_element_type=jnp.float32)
    silu_gate, sigma_gate = silu_parts(gate_pre)
    hidden = (silu_gate * up_pre).astype(jnp.bfloat16)
    return (gate_pre, up_pre, silu_gate, sigma_gate, hidden)


def backward_terms(grad_block, gate_pre, up_pre, silu_gate, sigma_gate, gate_w, up_w, down_w):
    dims = (((1,), (1,)), ((), ()))
    d_hidden = lax.dot_general(grad_block, down_w, dims, preferred_element_type=jnp.float32)
    d_gate = (d_hidden * up_pre * sigma_gate * (1.0 + gate_pre * (1.0 - sigma_gate))).astype(
        jnp.bfloat16
    )
    d_up = (d_hidden * silu_gate).astype(jnp.bfloat16)
    back_part = jnp.dot(d_gate, gate_w, preferred_element_type=jnp.float32) + jnp.dot(
        d_up, up_w, preferred_element_type=jnp.float32
    )
    return (d_gate, d_up, back_part)


def weight_grads(row_block, grad_block, hidden, d_gate, d_up):
    dims = (((0,), (0,)), ((), ()))
    grad_gate = lax.dot_general(d_gate, row_block, dims, preferred_element_type=jnp.float32).astype(
        jnp.bfloat16
    )
    grad_up = lax.dot_general(d_up, row_block, dims, preferred_element_type=jnp.float32).astype(
        jnp.bfloat16
    )
    grad_down = lax.dot_general(
        hidden, grad_block, dims, preferred_element_type=jnp.float32
    ).astype(jnp.bfloat16)
    return (grad_gate, grad_up, grad_down)


def per_device(tokens, cotangent, pick_lists, combine, w_gate, w_up, w_down):
    n_experts = lax.axis_size("expert")
    my_index = lax.axis_index("expert")
    tok_rows = tokens.shape[0]
    feat_width = tokens.shape[1]
    capacity = pick_lists.shape[2]
    slot_count = max(2, (2 * capacity + n_experts - 1) // n_experts)
    list_all = pick_lists[0]
    weight_all = combine[0]
    source_dev = list_all // tok_rows
    within_dev = list_all - source_dev * tok_rows
    is_mine = (source_dev == my_index).astype(jnp.int32)
    rank_mine = jnp.cumsum(is_mine, axis=1) - 1
    slot_ids = jnp.arange(slot_count, dtype=jnp.int32)
    select_mask = (is_mine[:, :, None] == 1) & (rank_mine[:, :, None] == slot_ids[None, None, :])
    select_int = select_mask.astype(jnp.int32)
    flat_row = jnp.sum(select_int * within_dev[:, :, None], axis=1).reshape(-1)
    flat_valid = (jnp.sum(select_int, axis=1) > 0).reshape(-1)
    flat_weight = jnp.sum(jnp.where(select_mask, weight_all[:, :, None], 0.0), axis=1).reshape(-1)
    slot_shape = (n_experts, slot_count, feat_width)
    row_send = jnp.where(
        flat_valid[:, None], jnp.take(tokens, flat_row, axis=0), jnp.zeros((), jnp.bfloat16)
    ).reshape(slot_shape)
    cot_rows = jnp.take(cotangent, flat_row, axis=0).astype(jnp.float32)
    grad_send = (
        jnp.where(flat_valid[:, None], flat_weight[:, None] * cot_rows, 0.0)
        .astype(jnp.bfloat16)
        .reshape(slot_shape)
    )
    own_source = lax.dynamic_index_in_dim(source_dev, my_index, 0, keepdims=False)
    order_ids = jnp.arange(capacity, dtype=jnp.int32)
    earlier = order_ids[:, None] > order_ids[None, :]
    same_source = own_source[:, None] == own_source[None, :]
    own_rank = jnp.sum((earlier & same_source).astype(jnp.int32), axis=1)
    position = own_source * slot_count + own_rank

    def compact(received):
        return jnp.take(received.reshape(n_experts * slot_count, feat_width), position, axis=0)

    def expand(result_rows):
        empty_slots = jnp.zeros((n_experts * slot_count, feat_width), jnp.bfloat16)
        return empty_slots.at[position].set(result_rows.astype(jnp.bfloat16)).reshape(slot_shape)

    gate_w = w_gate[0]
    up_w = w_up[0]
    down_w = w_down[0]
    recv_rows = lax.all_to_all(row_send, "expert", split_axis=0, concat_axis=0, tiled=True)
    row_block = lax.all_gather(compact(recv_rows), "dp", axis=0, tiled=True)
    gate_pre, up_pre, silu_gate, sigma_gate, hidden = project_hidden(row_block, gate_w, up_w)
    out_part = jnp.dot(hidden, down_w, preferred_element_type=jnp.float32)
    out_rows = lax.psum_scatter(
        out_part.astype(jnp.bfloat16), "dp", scatter_dimension=0, tiled=True
    ).astype(jnp.float32)
    out_slots = lax.all_to_all(expand(out_rows), "expert", split_axis=0, concat_axis=0, tiled=True)
    recv_grads = lax.all_to_all(grad_send, "expert", split_axis=0, concat_axis=0, tiled=True)
    grad_block = lax.all_gather(compact(recv_grads), "dp", axis=0, tiled=True)
    d_gate, d_up, back_part = backward_terms(
        grad_block, gate_pre, up_pre, silu_gate, sigma_gate, gate_w, up_w, down_w
    )
    back_rows = lax.psum_scatter(
        back_part.astype(jnp.bfloat16), "dp", scatter_dimension=0, tiled=True
    ).astype(jnp.float32)
    back_slots = lax.all_to_all(
        expand(back_rows), "expert", split_axis=0, concat_axis=0, tiled=True
    )
    grad_gate, grad_up, grad_down = weight_grads(row_block, grad_block, hidden, d_gate, d_up)
    out_flat = jnp.where(
        flat_valid[:, None],
        flat_weight[:, None] * out_slots.reshape(-1, feat_width).astype(jnp.float32),
        0.0,
    )
    layer_out = (
        jnp.zeros((tok_rows, feat_width), jnp.float32)
        .at[flat_row]
        .add(out_flat)
        .astype(jnp.bfloat16)
    )
    back_flat = jnp.where(
        flat_valid[:, None], back_slots.reshape(-1, feat_width).astype(jnp.float32), 0.0
    )
    tokens_grad = (
        jnp.zeros((tok_rows, feat_width), jnp.float32)
        .at[flat_row]
        .add(back_flat)
        .astype(jnp.bfloat16)
    )
    return (layer_out, tokens_grad, grad_gate[None], grad_up[None], grad_down[None])


def solution(mesh):
    placed = (
        P(("dp", "expert"), None),
        P(("dp", "expert"), None),
        P("dp", None, None),
        P("dp", None, None),
        P("expert", "dp", None),
        P("expert", "dp", None),
        P("expert", "dp", None),
    )
    return jax.shard_map(
        per_device,
        mesh=mesh,
        in_specs=placed,
        out_specs=(
            P(("dp", "expert"), None),
            P(("dp", "expert"), None),
            P("expert", "dp", None),
            P("expert", "dp", None),
            P("expert", "dp", None),
        ),
        check_vma=False,
    )
```

profile of v0, /device:TPU:1, one launch (start us, length us, event | category | flops | bytes accessed | tf_op | source)
XLA Modules:
  0.0 480.7 jit_solution(4581792306209189560)
XLA Ops:
  7.2 0.0 copy-start
  7.2 0.8 broadcast_compare_fusion
  8.0 0.3 reduce_window_sum.11
  8.3 0.8 add_select_fusion
  9.1 0.2 convert_reduce_fusion
  9.3 0.1 copy.12
  9.4 0.1 reshape.199
  9.6 0.9 select_reduce_fusion
  10.5 0.1 copy.13
  10.6 0.1 gt.25
  10.7 0.1 copy.14
  10.8 0.1 mul.76
  10.9 1.2 gather_fusion.2
  12.1 0.3 select_convert_fusion
  12.4 1.0 reshape.203
  13.4 14.6 %all-to-all-start.2 = ((bf16[64,4,1024]{2,1,0:T(4,128)(2,1)}), bf16[64,4,1024]{2,1,0:T(4,128)(2,1)S(1)}, u32[]{:S(2)}, u32[]{:S(2)}) async-start(bf16[64,4,1024]{2,1,0:T(4,128)(2,1)} %reshape.203), calls=%async_computation.3 | async-start | bytes 1048576 | tf_op jit(solution)/shard_map/all_to_all | solution.py:102
  28.0 1.2 gather_fusion
  29.1 0.1 select_select_fusion
  29.3 1.0 reshape.200
  30.3 15.4 %all-to-all-done.2 = bf16[64,4,1024]{2,1,0:T(4,128)(2,1)S(1)} async-done(((bf16[64,4,1024]{2,1,0:T(4,128)(2,1)}), bf16[64,4,1024]{2,1,0:T(4,128)(2,1)S(1)}, u32[]{:S(2)}, u32[]{:S(2)}) %all-to-all-start.2) | async-done | bytes 524320 | tf_op jit(solution)/shard_map/all_to_all | solution.py:102
  45.6 5.6 %all-to-all-start = ((bf16[64,4,1024]{2,1,0:T(4,128)(2,1)}), bf16[64,4,1024]{2,1,0:T(4,128)(2,1)S(1)}, u32[]{:S(2)}, u32[]{:S(2)}) async-start(bf16[64,4,1024]{2,1,0:T(4,128)(2,1)} %reshape.200), calls=%async_computation | async-start | bytes 1048576 | tf_op jit(solution)/shard_map/all_to_all | solution.py:94
  51.2 0.0 all-gather.3.cloned.1.call-start
  51.3 0.2 convert_reduce_fusion.1
  51.5 0.1 reshape.204
  51.6 0.9 gather_fusion.3
  52.5 16.4 %all-to-all-done = bf16[64,4,1024]{2,1,0:T(4,128)(2,1)S(1)} async-done(((bf16[64,4,1024]{2,1,0:T(4,128)(2,1)}), bf16[64,4,1024]{2,1,0:T(4,128)(2,1)S(1)}, u32[]{:S(2)}, u32[]{:S(2)}) %all-to-all-start) | async-done | bytes 524320 | tf_op jit(solution)/shard_map/all_to_all | solution.py:94
  68.9 0.1 reshape.201
  69.1 0.9 gather_fusion.1
  69.9 0.9 broadcast_select_fusion
  70.8 0.0 all-gather.3.cloned.1.call-update
  70.9 0.0 all-gather.5.cloned.1.call-start
  70.9 0.7 all-gather.5.cloned.1.call-update
  71.6 0.0 reduce-scatter.3.cloned.1.call-start
  71.7 78.6 %all-gather.3.cloned.1.call-done = bf16[1024,1024]{1,0:T(8,128)(2,1)} async-done(((bf16[128,1024]{1,0:T(8,128)(2,1)}), bf16[1024,1024]{1,0:T(8,128)(2,1)}) %all-gather.3.cloned.1.call-update) | async-done | bytes 2097168 | tf_op jit(solution)/shard_map/all_gather | solution.py:95
  150.3 3.3 fusion.18
  153.6 1.5 fusion.22
  155.1 76.9 %all-gather.5.cloned.1.call-done = bf16[1024,1024]{1,0:T(8,128)(2,1)} async-done(((bf16[128,1024]{1,0:T(8,128)(2,1)}), bf16[1024,1024]{1,0:T(8,128)(2,1)}) %all-gather.5.cloned.1.call-update) | async-done | bytes 2097168 | tf_op jit(solution)/shard_map/all_gather | solution.py:103
  232.0 2.6 multiply_convert_fusion
  234.7 0.7 copy-done.6
  235.3 2.0 convolution_convert_fusion
  237.3 0.0 reduce-scatter.3.cloned.1.call-update
  237.4 0.0 reduce-scatter.5.cloned.1.call-start
  237.4 0.7 fusion.20
  238.1 2.0 add_convert_fusion
  240.1 0.0 reduce-scatter.5.cloned.1.call-update
  240.2 94.4 %reduce-scatter.3.cloned.1.call-done = bf16[128,1024]{1,0:T(8,128)(2,1)} async-done(((bf16[1024,1024]{1,0:T(8,128)(2,1)}), bf16[128,1024]{1,0:T(8,128)(2,1)}) %reduce-scatter.3.cloned.1.call-update) | async-done | bytes 262160 | tf_op jit(solution)/shard_map/reduce_scatter | solution.py:98
  334.6 1.7 scatter_custom_fusion
  336.3 1.0 reshape.202
  337.3 10.0 %all-to-all-start.1 = ((bf16[64,4,1024]{2,1,0:T(4,128)(2,1)}), bf16[64,4,1024]{2,1,0:T(4,128)(2,1)S(1)}, u32[]{:S(2)}, u32[]{:S(2)}) async-start(bf16[64,4,1024]{2,1,0:T(4,128)(2,1)} %reshape.202), calls=%async_computation.2 | async-start | bytes 1048576 | tf_op jit(solution)/shard_map/all_to_all | solution.py:101
  347.3 92.8 %reduce-scatter.5.cloned.1.call-done = bf16[128,1024]{1,0:T(8,128)(2,1)} async-done(((bf16[1024,1024]{1,0:T(8,128)(2,1)}), bf16[128,1024]{1,0:T(8,128)(2,1)}) %reduce-scatter.5.cloned.1.call-update) | async-done | bytes 262160 | tf_op jit(solution)/shard_map/reduce_scatter | solution.py:107
  440.1 1.7 scatter_custom_fusion.2
  441.8 1.0 reshape.205
  442.8 9.9 %all-to-all-start.3 = ((bf16[64,4,1024]{2,1,0:T(4,128)(2,1)}), bf16[64,4,1024]{2,1,0:T(4,128)(2,1)S(1)}, u32[]{:S(2)}, u32[]{:S(2)}) async-start(bf16[64,4,1024]{2,1,0:T(4,128)(2,1)} %reshape.205), calls=%async_computation.5 | async-start | bytes 1048576 | tf_op jit(solution)/shard_map/all_to_all | solution.py:110
  452.7 0.1 reshape.198
  452.9 2.9 fusion.2
  455.8 1.2 fusion.1
  457.0 1.2 fusion
  458.2 0.1 reshape.206
  458.2 2.9 scatter_custom_fusion.1
  461.2 0.7 convert_element_type.76
  461.9 8.5 %all-to-all-done.3 = bf16[64,4,1024]{2,1,0:T(4,128)(2,1)S(1)} async-done(((bf16[64,4,1024]{2,1,0:T(4,128)(2,1)}), bf16[64,4,1024]{2,1,0:T(4,128)(2,1)S(1)}, u32[]{:S(2)}, u32[]{:S(2)}) %all-to-all-start.3) | async-done | bytes 524320 | tf_op jit(solution)/shard_map/all_to_all | solution.py:110
  470.4 0.1 reshape.207
  470.5 2.9 scatter_custom_fusion.3
  473.4 0.7 convert_element_type.84
  (30 shorter events, 0.1 us)
Async XLA Ops:
  7.2 224.8 %copy-start = (bf16[1,128,1024]{2,1,0:T(8,128)(2,1)S(1)}, bf16[1,128,1024]{2,1,0:T(8,128)(2,1)}, u32[]{:S(2)}) copy-start(bf16[1,128,1024]{2,1,0:T(8,128)(2,1)} %param.17) | copy-start | bytes 786436
  7.2 3.7 copy-start.1
  12.1 15.9 %copy-start.2 = (bf16[128,1024]{1,0:T(8,128)(2,1)S(1)}, bf16[128,1024]{1,0:T(8,128)(2,1)}, u32[]{:S(2)}) copy-start(bf16[128,1024]{1,0:T(8,128)(2,1)} %param.11) | copy-start | bytes 786436
  13.4 32.3 %all-to-all-start.2 = ((bf16[64,4,1024]{2,1,0:T(4,128)(2,1)}), bf16[64,4,1024]{2,1,0:T(4,128)(2,1)S(1)}, u32[]{:S(2)}, u32[]{:S(2)}) async-start(bf16[64,4,1024]{2,1,0:T(4,128)(2,1)} %reshape.203), calls=%async_computation.3 | async-start | bytes 1048576 | tf_op jit(solution)/shard_map/all_to_all | solution.py:102
  45.6 23.3 %all-to-all-start = ((bf16[64,4,1024]{2,1,0:T(4,128)(2,1)}), bf16[64,4,1024]{2,1,0:T(4,128)(2,1)S(1)}, u32[]{:S(2)}, u32[]{:S(2)}) async-start(bf16[64,4,1024]{2,1,0:T(4,128)(2,1)} %reshape.200), calls=%async_computation | async-start | bytes 1048576 | tf_op jit(solution)/shard_map/all_to_all | solution.py:94
  51.2 99.1 %all-gather.3.cloned.1.call-start = ((), (), s32[]{:S(2)}) async-start(), calls=%async_computation.6 | async-start | bytes 2359296 | tf_op jit(solution)/shard_map/all_gather | solution.py:95
  69.0 81.2 %copy-start.10 = (bf16[1,128,1024]{2,1,0:T(8,128)(2,1)S(1)}, bf16[1,128,1024]{2,1,0:T(8,128)(2,1)}, u32[]{:S(2)}) copy-start(bf16[1,128,1024]{2,1,0:T(8,128)(2,1)} %param.16) | copy-start | bytes 786436
  69.9 83.6 %copy-start.7 = (bf16[1,128,1024]{2,1,0:T(8,128)(2,1)S(1)}, bf16[1,128,1024]{2,1,0:T(8,128)(2,1)}, u32[]{:S(2)}) copy-start(bf16[1,128,1024]{2,1,0:T(8,128)(2,1)} %param.15) | copy-start | bytes 786436
  70.9 161.1 %all-gather.5.cloned.1.call-start = ((), (), s32[]{:S(2)}) async-start(), calls=%async_computation.8 | async-start | bytes 2359296 | tf_op jit(solution)/shard_map/all_gather | solution.py:103
  71.6 263.0 %reduce-scatter.3.cloned.1.call-start = ((), (), s32[]{:S(2)}) async-start(), calls=%async_computation.7 | async-start | bytes 2359296 | tf_op jit(solution)/shard_map/reduce_scatter | solution.py:98
  150.3 3.3 copy-start.3
  234.6 0.7 copy-start.6
  234.6 2.8 copy-start.4
  234.6 3.5 copy-start.8
  237.4 202.7 %reduce-scatter.5.cloned.1.call-start = ((), (), s32[]{:S(2)}) async-start(), calls=%async_computation.9 | async-start | bytes 2359296 | tf_op jit(solution)/shard_map/reduce_scatter | solution.py:107
  337.3 105.5 %all-to-all-start.1 = ((bf16[64,4,1024]{2,1,0:T(4,128)(2,1)}), bf16[64,4,1024]{2,1,0:T(4,128)(2,1)S(1)}, u32[]{:S(2)}, u32[]{:S(2)}) async-start(bf16[64,4,1024]{2,1,0:T(4,128)(2,1)} %reshape.202), calls=%async_computation.2 | async-start | bytes 1048576 | tf_op jit(solution)/shard_map/all_to_all | solution.py:101
  442.8 27.6 %all-to-all-start.3 = ((bf16[64,4,1024]{2,1,0:T(4,128)(2,1)}), bf16[64,4,1024]{2,1,0:T(4,128)(2,1)S(1)}, u32[]{:S(2)}, u32[]{:S(2)}) async-start(bf16[64,4,1024]{2,1,0:T(4,128)(2,1)} %reshape.205), calls=%async_computation.5 | async-start | bytes 1048576 | tf_op jit(solution)/shard_map/all_to_all | solution.py:110
  452.8 3.0 copy-start.9
  452.9 4.1 copy-start.5
Sparse Core Ops, SparseCore 0:
  71.0 79.2 all-gather.2
  154.1 77.8 all-gather.4
  237.5 97.0 reduce-scatter.2
  339.1 100.9 reduce-scatter.4
where the time goes:
time: 481 us
  waiting for transfers between devices  384 us (80%)
  starting transfers between devices  40.2 us (8%)
  matrix products  17.4 us (4%)
  between operations  14.1 us (3%)
  local copies, waits for them, and re-layouts  13.3 us (3%)
  other arithmetic  11.8 us (2%)
    reduce_scatter x1, waiting for transfers between devices, per_device(): lax.psum_scatter(out_part.astype(jnp.bfloat16), 'dp', scatter_dimension=0...  94.4 us
    reduce_scatter x1, waiting for transfers between devices, per_device(): lax.psum_scatter(back_part.astype(jnp.bfloat16), 'dp', scatter_dimension=...  92.8 us
    all_gather x1, waiting for transfers between devices, per_device(): row_block = lax.all_gather(compact(recv_rows), 'dp', axis=0, tiled=True)  78.6 us
    all_gather x1, waiting for transfers between devices, per_device(): grad_block = lax.all_gather(compact(recv_grads), 'dp', axis=0, tiled=True)  76.9 us
    all_to_all x1, waiting for transfers between devices, per_device(): lax.all_to_all(row_send, 'expert', split_axis=0, concat_axis=0, tiled=True)  16.4 us
    all_to_all x1, waiting for transfers between devices, per_device(): lax.all_to_all(grad_send, 'expert', split_axis=0, concat_axis=0, tiled=True)  15.4 us
    all_to_all x1, starting transfers between devices, per_device(): lax.all_to_all(grad_send, 'expert', split_axis=0, concat_axis=0, tiled=True)  14.6 us
    all_to_all x1, starting transfers between devices, per_device(): lax.all_to_all(expand(out_rows), 'expert', split_axis=0, concat_axis=0, t...  9.97 us
  transfers between devices with their start and end apart: 8, of which 7 were waited for; matrix products, arithmetic and copies ran while one was open for 5% of the time, Pallas kernels for 0%

commit v1 on v0

--- a/solution.py
+++ b/solution.py
@@ -92,7 +92,9 @@
     up_w = w_up[0]
     down_w = w_down[0]
     recv_rows = lax.all_to_all(row_send, "expert", split_axis=0, concat_axis=0, tiled=True)
-    row_block = lax.all_gather(compact(recv_rows), "dp", axis=0, tiled=True)
+    row_block = jnp.concatenate(
+        lax.all_to_all(jnp.stack([compact(recv_rows)] * lax.axis_size("dp")), "dp", 0, 0), axis=0
+    )
     gate_pre, up_pre, silu_gate, sigma_gate, hidden = project_hidden(row_block, gate_w, up_w)
     out_part = jnp.dot(hidden, down_w, preferred_element_type=jnp.float32)
     out_rows = lax.psum_scatter(

time: 481 us -> 432 us (0.90)
  waiting for transfers between devices: 384 us -> 325 us
  starting transfers between devices: 40.2 us -> 50.1 us
    all_gather x1 -> x0, waiting for transfers between devices: 78.6 us -> none  [per_device(): row_block = lax.all_gather(compact(recv_rows), 'dp', axis=0, tiled=True)]
    all_to_all x0 -> x1, waiting for transfers between devices: none -> 34.3 us  [per_device(): lax.all_to_all(jnp.stack([compact(recv_rows)] * lax.axis_size('dp')), 'dp...]
    all_gather x1, waiting for transfers between devices: 76.9 us -> 61.9 us  [per_device(): grad_block = lax.all_gather(compact(recv_grads), 'dp', axis=0, tiled=True)]
    all_to_all x0 -> x1, starting transfers between devices: none -> 9.9 us  [per_device(): lax.all_to_all(jnp.stack([compact(recv_rows)] * lax.axis_size('dp')), 'dp...]
where the time goes in v1:
time: 432 us; the launch traced here: 431 us
  waiting for transfers between devices  325 us (75%)
  starting transfers between devices  50.1 us (12%)
  matrix products  15 us (3%)
  local copies, waits for them, and re-layouts  14.9 us (3%)
  between operations  14.1 us (3%)
  other arithmetic  11.7 us (3%)
    reduce_scatter x1, waiting for transfers between devices, per_device(): lax.psum_scatter(out_part.astype(jnp.bfloat16), 'dp', scatter_dimension=0...  94.7 us
    reduce_scatter x1, waiting for transfers between devices, per_device(): lax.psum_scatter(back_part.astype(jnp.bfloat16), 'dp', scatter_dimension=...  92.6 us
    all_gather x1, waiting for transfers between devices, per_device(): grad_block = lax.all_gather(compact(recv_grads), 'dp', axis=0, tiled=True)  61.9 us
    all_to_all x1, waiting for transfers between devices, per_device(): lax.all_to_all(jnp.stack([compact(recv_rows)] * lax.axis_size('dp')), 'dp...  34.3 us
    all_to_all x1, waiting for transfers between devices, per_device(): lax.all_to_all(row_send, 'expert', split_axis=0, concat_axis=0, tiled=True)  16.5 us
    all_to_all x1, waiting for transfers between devices, per_device(): lax.all_to_all(grad_send, 'expert', split_axis=0, concat_axis=0, tiled=True)  15.4 us
    all_to_all x1, starting transfers between devices, per_device(): lax.all_to_all(grad_send, 'expert', split_axis=0, concat_axis=0, tiled=True)  14.6 us
    all_to_all x1, starting transfers between devices, per_device(): lax.all_to_all(expand(back_rows), 'expert', split_axis=0, concat_axis=0,...  9.98 us
  transfers between devices with their start and end apart: 8, of which 7 were waited for; matrix products, arithmetic and copies ran while one was open for 5% of the time, Pallas kernels for 0%

profile of v1, /device:TPU:1, one launch (start us, length us, event | category | flops | bytes accessed | tf_op | source)
XLA Modules:
  0.0 431.1 jit_solution(11905214743651437053)
XLA Ops:
  7.2 0.0 copy-start
  7.2 0.8 broadcast_compare_fusion
  8.0 0.3 reduce_window_sum.11
  8.3 0.8 add_select_fusion
  9.1 0.2 convert_reduce_fusion
  9.3 0.1 copy.12
  9.4 0.1 reshape.204
  9.6 0.9 select_reduce_fusion
  10.5 0.1 copy.13
  10.6 0.1 gt.25
  10.7 0.1 copy.14
  10.8 0.1 mul.76
  10.9 1.2 gather_fusion.2
  12.1 0.3 select_convert_fusion
  12.4 1.0 reshape.209
  13.4 14.6 %all-to-all-start.3 = ((bf16[64,4,1024]{2,1,0:T(4,128)(2,1)}), bf16[64,4,1024]{2,1,0:T(4,128)(2,1)S(1)}, u32[]{:S(2)}, u32[]{:S(2)}) async-start(bf16[64,4,1024]{2,1,0:T(4,128)(2,1)} %reshape.209), calls=%async_computation.4 | async-start | bytes 1048576 | tf_op jit(solution)/shard_map/all_to_all | solution.py:104
  28.0 1.2 gather_fusion
  29.1 0.1 select_select_fusion
  29.3 1.0 reshape.205
  30.3 15.4 %all-to-all-done.3 = bf16[64,4,1024]{2,1,0:T(4,128)(2,1)S(1)} async-done(((bf16[64,4,1024]{2,1,0:T(4,128)(2,1)}), bf16[64,4,1024]{2,1,0:T(4,128)(2,1)S(1)}, u32[]{:S(2)}, u32[]{:S(2)}) %all-to-all-start.3) | async-done | bytes 524320 | tf_op jit(solution)/shard_map/all_to_all | solution.py:104
  45.6 5.6 %all-to-all-start = ((bf16[64,4,1024]{2,1,0:T(4,128)(2,1)}), bf16[64,4,1024]{2,1,0:T(4,128)(2,1)S(1)}, u32[]{:S(2)}, u32[]{:S(2)}) async-start(bf16[64,4,1024]{2,1,0:T(4,128)(2,1)} %reshape.205), calls=%async_computation | async-start | bytes 1048576 | tf_op jit(solution)/shard_map/all_to_all | solution.py:94
  51.2 0.2 convert_reduce_fusion.1
  51.5 0.1 reshape.210
  51.6 0.9 gather_fusion.3
  52.4 16.5 %all-to-all-done = bf16[64,4,1024]{2,1,0:T(4,128)(2,1)S(1)} async-done(((bf16[64,4,1024]{2,1,0:T(4,128)(2,1)}), bf16[64,4,1024]{2,1,0:T(4,128)(2,1)S(1)}, u32[]{:S(2)}, u32[]{:S(2)}) %all-to-all-start) | async-done | bytes 524320 | tf_op jit(solution)/shard_map/all_to_all | solution.py:94
  68.9 0.1 reshape.206
  69.0 0.9 gather_fusion.1
  69.9 0.8 broadcast_select_fusion
  70.7 1.6 stack.2
  72.3 9.9 %all-to-all-start.1 = ((bf16[8,128,1024]{2,1,0:T(8,128)(2,1)}), bf16[8,128,1024]{2,1,0:T(8,128)(2,1)S(1)}, u32[]{:S(2)}, u32[]{:S(2)}) async-start(bf16[8,128,1024]{2,1,0:T(8,128)(2,1)} %stack.2), calls=%async_computation.1 | async-start | bytes 4194304 | tf_op jit(solution)/shard_map/all_to_all | solution.py:96
  82.2 0.0 all-gather.2.cloned.1.call-start
  82.2 0.7 all-gather.2.cloned.1.call-update
  82.9 0.0 reduce-scatter.3.cloned.1.call-start
  83.0 34.3 %all-to-all-done.1 = bf16[8,128,1024]{2,1,0:T(8,128)(2,1)S(1)} async-done(((bf16[8,128,1024]{2,1,0:T(8,128)(2,1)}), bf16[8,128,1024]{2,1,0:T(8,128)(2,1)S(1)}, u32[]{:S(2)}, u32[]{:S(2)}) %all-to-all-start.1) | async-done | bytes 2097184 | tf_op jit(solution)/shard_map/all_to_all | solution.py:96
  117.3 1.5 fusion.18
  118.8 1.5 fusion.22
  120.3 61.9 %all-gather.2.cloned.1.call-done = bf16[1024,1024]{1,0:T(8,128)(2,1)} async-done(((bf16[128,1024]{1,0:T(8,128)(2,1)}), bf16[1024,1024]{1,0:T(8,128)(2,1)}) %all-gather.2.cloned.1.call-update) | async-done | bytes 2097168 | tf_op jit(solution)/shard_map/all_gather | solution.py:105
  182.2 2.6 multiply_convert_fusion
  184.8 0.7 copy-done.4
  185.5 2.0 convolution_convert_fusion
  187.5 0.0 reduce-scatter.3.cloned.1.call-update
  187.5 0.0 reduce-scatter.5.cloned.1.call-start
  187.6 0.7 fusion.20
  188.3 2.0 add_convert_fusion
  190.3 0.0 reduce-scatter.5.cloned.1.call-update
  190.3 94.7 %reduce-scatter.3.cloned.1.call-done = bf16[128,1024]{1,0:T(8,128)(2,1)} async-done(((bf16[1024,1024]{1,0:T(8,128)(2,1)}), bf16[128,1024]{1,0:T(8,128)(2,1)}) %reduce-scatter.3.cloned.1.call-update) | async-done | bytes 262160 | tf_op jit(solution)/shard_map/reduce_scatter | solution.py:100
  285.1 1.7 scatter_custom_fusion
  286.8 1.0 reshape.208
  287.8 10.0 %all-to-all-start.2 = ((bf16[64,4,1024]{2,1,0:T(4,128)(2,1)}), bf16[64,4,1024]{2,1,0:T(4,128)(2,1)S(1)}, u32[]{:S(2)}, u32[]{:S(2)}) async-start(bf16[64,4,1024]{2,1,0:T(4,128)(2,1)} %reshape.208), calls=%async_computation.3 | async-start | bytes 1048576 | tf_op jit(solution)/shard_map/all_to_all | solution.py:103
  297.8 92.6 %reduce-scatter.5.cloned.1.call-done = bf16[128,1024]{1,0:T(8,128)(2,1)} async-done(((bf16[1024,1024]{1,0:T(8,128)(2,1)}), bf16[128,1024]{1,0:T(8,128)(2,1)}) %reduce-scatter.5.cloned.1.call-update) | async-done | bytes 262160 | tf_op jit(solution)/shard_map/reduce_scatter | solution.py:109
  390.4 1.7 scatter_custom_fusion.2
  392.2 1.0 reshape.211
  393.1 10.0 %all-to-all-start.4 = ((bf16[64,4,1024]{2,1,0:T(4,128)(2,1)}), bf16[64,4,1024]{2,1,0:T(4,128)(2,1)S(1)}, u32[]{:S(2)}, u32[]{:S(2)}) async-start(bf16[64,4,1024]{2,1,0:T(4,128)(2,1)} %reshape.211), calls=%async_computation.6 | async-start | bytes 1048576 | tf_op jit(solution)/shard_map/all_to_all | solution.py:112
  403.1 0.1 reshape.203
  403.3 2.3 fusion.1
  405.6 1.2 fusion
  406.7 1.2 fusion.2
  407.9 0.1 reshape.212
  408.0 2.9 scatter_custom_fusion.1
  410.9 0.7 convert_element_type.76
  411.7 9.2 %all-to-all-done.4 = bf16[64,4,1024]{2,1,0:T(4,128)(2,1)S(1)} async-done(((bf16[64,4,1024]{2,1,0:T(4,128)(2,1)}), bf16[64,4,1024]{2,1,0:T(4,128)(2,1)S(1)}, u32[]{:S(2)}, u32[]{:S(2)}) %all-to-all-start.4) | async-done | bytes 524320 | tf_op jit(solution)/shard_map/all_to_all | solution.py:112
  420.8 0.1 reshape.213
  420.9 2.9 scatter_custom_fusion.3
  423.8 0.7 convert_element_type.84
  (30 shorter events, 0.1 us)
Async XLA Ops:
  7.2 175.0 %copy-start = (bf16[1,128,1024]{2,1,0:T(8,128)(2,1)S(1)}, bf16[1,128,1024]{2,1,0:T(8,128)(2,1)}, u32[]{:S(2)}) copy-start(bf16[1,128,1024]{2,1,0:T(8,128)(2,1)} %param.17) | copy-start | bytes 786436
  7.2 3.7 copy-start.1
  12.1 15.8 %copy-start.2 = (bf16[128,1024]{1,0:T(8,128)(2,1)S(1)}, bf16[128,1024]{1,0:T(8,128)(2,1)}, u32[]{:S(2)}) copy-start(bf16[128,1024]{1,0:T(8,128)(2,1)} %param.11) | copy-start | bytes 786436
  13.4 32.3 %all-to-all-start.3 = ((bf16[64,4,1024]{2,1,0:T(4,128)(2,1)}), bf16[64,4,1024]{2,1,0:T(4,128)(2,1)S(1)}, u32[]{:S(2)}, u32[]{:S(2)}) async-start(bf16[64,4,1024]{2,1,0:T(4,128)(2,1)} %reshape.209), calls=%async_computation.4 | async-start | bytes 1048576 | tf_op jit(solution)/shard_map/all_to_all | solution.py:104
  45.6 23.3 %all-to-all-start = ((bf16[64,4,1024]{2,1,0:T(4,128)(2,1)}), bf16[64,4,1024]{2,1,0:T(4,128)(2,1)S(1)}, u32[]{:S(2)}, u32[]{:S(2)}) async-start(bf16[64,4,1024]{2,1,0:T(4,128)(2,1)} %reshape.205), calls=%async_computation | async-start | bytes 1048576 | tf_op jit(solution)/shard_map/all_to_all | solution.py:94
  72.3 45.0 %copy-start.10 = (bf16[1,128,1024]{2,1,0:T(8,128)(2,1)S(1)}, bf16[1,128,1024]{2,1,0:T(8,128)(2,1)}, u32[]{:S(2)}) copy-start(bf16[1,128,1024]{2,1,0:T(8,128)(2,1)} %param.16) | copy-start | bytes 786436
  72.3 45.0 %all-to-all-start.1 = ((bf16[8,128,1024]{2,1,0:T(8,128)(2,1)}), bf16[8,128,1024]{2,1,0:T(8,128)(2,1)S(1)}, u32[]{:S(2)}, u32[]{:S(2)}) async-start(bf16[8,128,1024]{2,1,0:T(8,128)(2,1)} %stack.2), calls=%async_computation.1 | async-start | bytes 4194304 | tf_op jit(solution)/shard_map/all_to_all | solution.py:96
  82.2 36.6 %copy-start.8 = (bf16[1,128,1024]{2,1,0:T(8,128)(2,1)S(1)}, bf16[1,128,1024]{2,1,0:T(8,128)(2,1)}, u32[]{:S(2)}) copy-start(bf16[1,128,1024]{2,1,0:T(8,128)(2,1)} %param.15) | copy-start | bytes 786436
  82.2 100.0 %all-gather.2.cloned.1.call-start = ((), (), s32[]{:S(2)}) async-start(), calls=%async_computation.8 | async-start | bytes 2359296 | tf_op jit(solution)/shard_map/all_gather | solution.py:105
  82.9 202.1 %reduce-scatter.3.cloned.1.call-start = ((), (), s32[]{:S(2)}) async-start(), calls=%async_computation.7 | async-start | bytes 2359296 | tf_op jit(solution)/shard_map/reduce_scatter | solution.py:100
  184.8 0.7 copy-start.4
  184.8 2.8 copy-start.6
  184.8 3.5 copy-start.9
  187.5 202.9 %reduce-scatter.5.cloned.1.call-start = ((), (), s32[]{:S(2)}) async-start(), calls=%async_computation.9 | async-start | bytes 2359296 | tf_op jit(solution)/shard_map/reduce_scatter | solution.py:109
  287.8 105.3 %all-to-all-start.2 = ((bf16[64,4,1024]{2,1,0:T(4,128)(2,1)}), bf16[64,4,1024]{2,1,0:T(4,128)(2,1)S(1)}, u32[]{:S(2)}, u32[]{:S(2)}) async-start(bf16[64,4,1024]{2,1,0:T(4,128)(2,1)} %reshape.208), calls=%async_computation.3 | async-start | bytes 1048576 | tf_op jit(solution)/shard_map/all_to_all | solution.py:103
  393.1 27.7 %all-to-all-start.4 = ((bf16[64,4,1024]{2,1,0:T(4,128)(2,1)}), bf16[64,4,1024]{2,1,0:T(4,128)(2,1)S(1)}, u32[]{:S(2)}, u32[]{:S(2)}) async-start(bf16[64,4,1024]{2,1,0:T(4,128)(2,1)} %reshape.211), calls=%async_computation.6 | async-start | bytes 1048576 | tf_op jit(solution)/shard_map/all_to_all | solution.py:112
  403.2 2.3 copy-start.7
  403.3 3.5 copy-start.3
  403.3 3.5 copy-start.5
Sparse Core Ops, SparseCore 0:
  86.8 95.3 all-gather.1
  187.7 97.3 reduce-scatter.2
  289.7 100.6 reduce-scatter.4
